TPU v7x, 32 devices: a whole 2x2x4 slice. The times are simulated.
32 devices in a mesh: section: 2 (over core), expert: 8 (over z, x), dp: 2 (over y).
Axes of the slice: x: 2, y: 2, z: 4, core: 2. Of those that a mesh axis runs over, the one named last changes fastest.
Arguments:
- tokens: bfloat16 [4, 512, 2048], P(None, ('expert', 'dp')), may hold values from -6 to 6
- routes: int32 [2, 4, 512, 2], P('section', None, ('expert', 'dp')), may hold values from 0 to 7, all different within a row; in each aligned block of 32 rows (0 to 31, 32 to 63, ..., all dimensions but the last counted through in order) at most 9 rows name the same one
- gate_probs: float32 [2, 4, 512, 2], P('section', None, ('expert', 'dp')), may hold values from 0.1 to 1
- w_gate: bfloat16 [2, 8, 2048, 640], P('section', 'expert'), may hold values from -0.125 to 0.125
- w_up: bfloat16 [2, 8, 2048, 640], P('section', 'expert'), may hold values from -0.125 to 0.125
- w_down: bfloat16 [2, 8, 640, 2048], P('section', 'expert'), may hold values from -0.25 to 0.25
- cotangent: bfloat16 [4, 512, 2048], P(None, ('expert', 'dp')), may hold values from -0.29882812 to 0.29882812
Outputs:
- grad_gate: float32 [2, 8, 2048, 640], P('section', 'expert', 'dp')
- grad_up: float32 [2, 8, 2048, 640], P('section', 'expert', 'dp')
- grad_down: float32 [2, 8, 640, 2048], P('section', 'expert', None, 'dp')
Inputs may be any that keep to these rules, and one draw needn't show every extreme that they name: `routes`: in each micro-batch and layer, the 32 token rows of one device (aligned blocks) name each expert at most 9 times, a bound that some block reaches; the 2 experts of a token differ.
All inputs are finite; a program needn't handle non-finite values.
Results may differ from a plain program's by a relative error of at most 0.015.
Values may be sent and summed in bfloat16 or wider, within the bound.
No kernel may reach another device: no remote copies, remote signals or barrier semaphores. Data moves between devices by JAX's collectives and lax.ppermute only.
A program may use at most 64 MiB of HBM per device.

v0:
```python
import jax
import jax.numpy as jnp
from jax import lax
from jax.sharding import PartitionSpec as P

epsilon = 1e-05
contract_rows = (((0,), (0,)), ((), ()))
contract_cols = (((1,), (1,)), ((), ()))


def shifted(value, axis, by):
    size = lax.axis_size(axis)
    pairs = [(i, i + by) for i in range(size) if 0 <= i + by < size]
    return lax.ppermute(value, axis, pairs)


def inverse_rms(values):
    return lax.rsqrt(jnp.mean(values * values, -1, keepdims=True) + epsilon)


def slot_selector(route_ids, experts, cap_slots):
    row_count, top_k = route_ids.shape
    flat_ids = route_ids.reshape(-1)
    one_hot = (flat_ids[:, None] == jnp.arange(experts, dtype=jnp.int32)[None, :]).astype(jnp.int32)
    earlier = jnp.cumsum(one_hot, 0) - one_hot
    slot_num = jnp.sum(earlier * one_hot, 1)
    target = (flat_ids * cap_slots + slot_num).reshape(row_count, top_k)
    columns = jnp.arange(experts * cap_slots, dtype=jnp.int32)
    return (target[:, :, None] == columns[None, None, :]).astype(jnp.bfloat16)


def keep_entry(store, value, position, is_live):
    previous = lax.dynamic_index_in_dim(store, position, 0, keepdims=False)
    return lax.dynamic_update_index_in_dim(store, jnp.where(is_live, value, previous), position, 0)


def shards(tokens, routes, gate_probs, w_gate, w_up, w_down, cotangent):
    micro_count, row_count, model_width = tokens.shape
    top_k = routes.shape[-1]
    experts = lax.axis_size("expert")
    sections = lax.axis_size("section")
    cap_slots = min(row_count, row_count * top_k // experts + 1)
    slot_rows = experts * cap_slots
    hidden = w_gate.shape[-1]
    section_pos = lax.axis_index("section")
    weight_gate = w_gate[0, 0]
    weight_up = w_up[0, 0]
    weight_down = w_down[0, 0]
    route_all = routes[0]
    prob_all = gate_probs[0]
    steps_total = micro_count + sections - 1

    def expert_forward(portion):
        leading = portion.shape[:-1]
        rows_flat = portion.reshape(-1, model_width)
        pre_gate = jnp.dot(rows_flat, weight_gate, preferred_element_type=jnp.float32)
        pre_up = jnp.dot(rows_flat, weight_up, preferred_element_type=jnp.float32)
        activation = (jax.nn.silu(pre_gate) * pre_up).astype(jnp.bfloat16)
        produced = jnp.dot(activation, weight_down, preferred_element_type=jnp.float32).astype(
            jnp.bfloat16
        )
        return (
            portion,
            pre_gate.reshape(leading + (hidden,)),
            pre_up.reshape(leading + (hidden,)),
            produced.reshape(portion.shape),
        )

    def forward_step(step_num, carried):
        incoming, keep_x, keep_rows, keep_gate, keep_up = carried
        micro_pos = step_num - section_pos
        is_live = (micro_pos >= 0) & (micro_pos < micro_count)
        position = jnp.clip(micro_pos, 0, micro_count - 1)
        fresh = lax.dynamic_index_in_dim(tokens, position, 0, keepdims=False)
        current = jnp.where(section_pos == 0, fresh, incoming)
        current_f = current.astype(jnp.float32)
        normed = (current_f * inverse_rms(current_f)).astype(jnp.bfloat16)
        route_ids = lax.dynamic_index_in_dim(route_all, position, 0, keepdims=False)
        probs = lax.dynamic_index_in_dim(prob_all, position, 0, keepdims=False)
        selector = slot_selector(route_ids, experts, cap_slots)
        outgoing = jnp.einsum(
            "rkj,rd->jd", selector, normed, preferred_element_type=jnp.float32
        ).astype(jnp.bfloat16)
        outgoing = outgoing.reshape(experts, cap_slots, model_width)
        received, pre_gate, pre_up, produced = expert_forward(
            lax.all_to_all(outgoing, "expert", split_axis=0, concat_axis=0, tiled=True)
        )
        returned = lax.all_to_all(produced, "expert", split_axis=0, concat_axis=0, tiled=True)
        chosen = jnp.einsum(
            "rkj,jd->rkd",
            selector,
            returned.reshape(slot_rows, model_width),
            preferred_element_type=jnp.float32,
        )
        mixed = (current_f + jnp.einsum("rk,rkd->rd", probs, chosen)).astype(jnp.bfloat16)
        keep_x = keep_entry(keep_x, current, position, is_live)
        keep_rows = keep_entry(
            keep_rows, received.reshape(slot_rows, model_width), position, is_live
        )
        keep_gate = keep_entry(keep_gate, pre_gate.reshape(slot_rows, hidden), position, is_live)
        keep_up = keep_entry(keep_up, pre_up.reshape(slot_rows, hidden), position, is_live)
        incoming = shifted(mixed, "section", 1)
        return (incoming, keep_x, keep_rows, keep_gate, keep_up)

    start_forward = (
        jnp.zeros((row_count, model_width), jnp.bfloat16),
        jnp.zeros((micro_count, row_count, model_width), jnp.bfloat16),
        jnp.zeros((micro_count, slot_rows, model_width), jnp.bfloat16),
        jnp.zeros((micro_count, slot_rows, hidden), jnp.float32),
        jnp.zeros((micro_count, slot_rows, hidden), jnp.float32),
    )
    finished = lax.fori_loop(0, steps_total, forward_step, start_forward)
    keep_x, keep_rows, keep_gate, keep_up = (finished[1], finished[2], finished[3], finished[4])

    def local_backward(operands):
        arrived, pre_gate, pre_up = operands
        back_hidden = lax.dot_general(
            arrived, weight_down, contract_cols, preferred_element_type=jnp.float32
        )
        sigmoid_gate = jax.nn.sigmoid(pre_gate)
        silu_gate = pre_gate * sigmoid_gate
        d_gate = (
            back_hidden * pre_up * sigmoid_gate * (1.0 + pre_gate * (1.0 - sigmoid_gate))
        ).astype(jnp.bfloat16)
        d_up = (back_hidden * silu_gate).astype(jnp.bfloat16)
        activation = (silu_gate * pre_up).astype(jnp.bfloat16)
        d_rows = (
            lax.dot_general(d_gate, weight_gate, contract_cols, preferred_element_type=jnp.float32)
            + lax.dot_general(d_up, weight_up, contract_cols, preferred_element_type=jnp.float32)
        ).astype(jnp.bfloat16)
        return (d_gate, d_up, activation, d_rows)

    def backward_step(step_num, carried):
        incoming, keep_go, keep_dgate, keep_dup, keep_act = carried
        micro_pos = step_num - (sections - 1 - section_pos)
        is_live = (micro_pos >= 0) & (micro_pos < micro_count)
        position = jnp.clip(micro_pos, 0, micro_count - 1)
        given_grad = lax.dynamic_index_in_dim(cotangent, position, 0, keepdims=False)
        upstream = jnp.where(section_pos == sections - 1, given_grad, incoming)
        upstream = jnp.where(is_live, upstream, jnp.zeros_like(upstream))
        upstream_f = upstream.astype(jnp.float32)
        current_f = lax.dynamic_index_in_dim(keep_x, position, 0, keepdims=False).astype(
            jnp.float32
        )
        route_ids = lax.dynamic_index_in_dim(route_all, position, 0, keepdims=False)
        probs = lax.dynamic_index_in_dim(prob_all, position, 0, keepdims=False)
        selector = slot_selector(route_ids, experts, cap_slots)
        scaled = (probs[:, :, None] * upstream_f[:, None, :]).astype(jnp.bfloat16)
        outgoing = jnp.einsum(
            "rkj,rkd->jd", selector, scaled, preferred_element_type=jnp.float32
        ).astype(jnp.bfloat16)
        arrived = lax.all_to_all(
            outgoing.reshape(experts, cap_slots, model_width),
            "expert",
            split_axis=0,
            concat_axis=0,
            tiled=True,
        )
        arrived = arrived.reshape(slot_rows, model_width)
        pre_gate = lax.dynamic_index_in_dim(keep_gate, position, 0, keepdims=False)
        pre_up = lax.dynamic_index_in_dim(keep_up, position, 0, keepdims=False)
        d_gate, d_up, activation, d_rows = local_backward((arrived, pre_gate, pre_up))
        sent_back = lax.all_to_all(
            d_rows.reshape(experts, cap_slots, model_width),
            "expert",
            split_axis=0,
            concat_axis=0,
            tiled=True,
        )
        d_normed = jnp.einsum(
            "rkj,jd->rd",
            selector,
            sent_back.reshape(slot_rows, model_width),
            preferred_element_type=jnp.float32,
        )
        scale_rms = inverse_rms(current_f)
        d_current = scale_rms * d_normed - current_f * scale_rms**3 * jnp.mean(
            d_normed * current_f, -1, keepdims=True
        )
        passed = (upstream_f + d_current).astype(jnp.bfloat16)
        keep_go = keep_entry(keep_go, arrived, position, is_live)
        keep_dgate = keep_entry(keep_dgate, d_gate, position, is_live)
        keep_dup = keep_entry(keep_dup, d_up, position, is_live)
        keep_act = keep_entry(keep_act, activation, position, is_live)
        incoming = shifted(passed, "section", -1)
        return (incoming, keep_go, keep_dgate, keep_dup, keep_act)

    start_backward = (
        jnp.zeros((row_count, model_width), jnp.bfloat16),
        jnp.zeros((micro_count, slot_rows, model_width), jnp.bfloat16),
        jnp.zeros((micro_count, slot_rows, hidden), jnp.bfloat16),
        jnp.zeros((micro_count, slot_rows, hidden), jnp.bfloat16),
        jnp.zeros((micro_count, slot_rows, hidden), jnp.bfloat16),
    )
    done = lax.fori_loop(0, steps_total, backward_step, start_backward)
    all_rows = micro_count * slot_rows
    rows_all = keep_rows.reshape(all_rows, model_width)
    go_all = done[1].reshape(all_rows, model_width)
    dgate_all = done[2].reshape(all_rows, hidden)
    dup_all = done[3].reshape(all_rows, hidden)
    act_all = done[4].reshape(all_rows, hidden)
    rows_part, go_part = (
        lax.all_to_all(rows_all, "dp", split_axis=1, concat_axis=0, tiled=True),
        lax.all_to_all(go_all, "dp", split_axis=1, concat_axis=0, tiled=True),
    )
    dgate_whole, dup_whole, act_whole = (
        lax.all_gather(dgate_all, "dp", axis=0, tiled=True),
        lax.all_gather(dup_all, "dp", axis=0, tiled=True),
        lax.all_gather(act_all, "dp", axis=0, tiled=True),
    )
    grad_gate = lax.dot_general(
        rows_part, dgate_whole, contract_rows, preferred_element_type=jnp.float32
    )
    grad_up = lax.dot_general(
        rows_part, dup_whole, contract_rows, preferred_element_type=jnp.float32
    )
    grad_down = lax.dot_general(
        act_whole, go_part, contract_rows, preferred_element_type=jnp.float32
    )
    return (grad_gate[None, None], grad_up[None, None], grad_down[None, None])


def solution(mesh):
    in_specs = (
        P(None, ("expert", "dp"), None),
        P("section", None, ("expert", "dp"), None),
        P("section", None, ("expert", "dp"), None),
        P("section", "expert", None, None),
        P("section", "expert", None, None),
        P("section", "expert", None, None),
        P(None, ("expert", "dp"), None),
    )
    out_specs = (
        P("section", "expert", "dp", None),
        P("section", "expert", "dp", None),
        P("section", "expert", None, "dp"),
    )
    return jax.shard_map(shards, mesh=mesh, in_specs=in_specs, out_specs=out_specs, check_vma=False)
```

profile of v0, /device:TPU:0, one launch (start us, length us, event | category | flops | bytes accessed | tf_op | source)
XLA Modules:
  0.0 650.3 jit_solution(5906262244409063740)
XLA Ops:
  5.2 266.9 %while.45 = (s32[]{:T(128)}, bf16[32,2048]{1,0:T(8,128)(2,1)S(1)}, bf16[4,32,2048]{2,1,0:T(8,128)(2,1)}, bf16[4,72,2048]{2,1,0:T(8,128)(2,1)}, f32[4,72,640]{2,1...) while((s32[]{:T(128)}, bf16[32,2048]{1,0:T(8,128)(2,1)S(1)}, ...), condition=%wide.region_5.6_spmd, body=%wide.region_0.5_spmd.sunk | while | flops 596245888 | bytes 43867772 | solution.py:112
  10.4 7.3 %all-to-all-start = ((bf16[8,9,2048]{2,1,0:T(8,128)(2,1)}), bf16[8,9,2048]{2,1,0:T(8,128)(2,1)S(1)}, u32[]{:S(2)}, u32[]{:S(2)}) async-start(bf16[8,9,2048]{2,1,0:T(8,128)(2,1)} %reshape.231), calls=%async_computation | async-start | bytes 1048576 | tf_op jit(solution)/shard_map/while/body/eval_jaxpr/all_to_all | solution.py:86
  19.5 12.7 %all-to-all-done = bf16[8,9,2048]{2,1,0:T(8,128)(2,1)S(1)} async-done(((bf16[8,9,2048]{2,1,0:T(8,128)(2,1)}), bf16[8,9,2048]{2,1,0:T(8,128)(2,1)S(1)}, u32[]{:S(2)}, u32[]{:S(2)}) %all-to-all-start) | async-done | bytes 294944 | tf_op jit(solution)/shard_map/while/body/eval_jaxpr/all_to_all | solution.py:86
  32.4 2.3 bitcast_dynamic-update-slice_fusion.11
  38.0 4.1 all-to-all-start.1
  42.5 14.0 %all-to-all-done.1 = bf16[8,9,2048]{2,1,0:T(8,128)(2,1)} async-done(((bf16[8,9,2048]{2,1,0:T(8,128)(2,1)}), bf16[8,9,2048]{2,1,0:T(8,128)(2,1)}, u32[]{:S(2)}, u32[]{:S(2)}) %all-to-all-start.1) | async-done | bytes 294944 | tf_op jit(solution)/shard_map/while/body/eval_jaxpr/all_to_all | solution.py:88
  66.7 4.1 all-to-all-start
  72.7 12.5 %all-to-all-done = bf16[8,9,2048]{2,1,0:T(8,128)(2,1)S(1)} async-done(((bf16[8,9,2048]{2,1,0:T(8,128)(2,1)}), bf16[8,9,2048]{2,1,0:T(8,128)(2,1)S(1)}, u32[]{:S(2)}, u32[]{:S(2)}) %all-to-all-start) | async-done | bytes 294944 | tf_op jit(solution)/shard_map/while/body/eval_jaxpr/all_to_all | solution.py:86
  85.3 2.3 bitcast_dynamic-update-slice_fusion.11
  90.9 4.1 all-to-all-start.1
  95.4 13.8 %all-to-all-done.1 = bf16[8,9,2048]{2,1,0:T(8,128)(2,1)} async-done(((bf16[8,9,2048]{2,1,0:T(8,128)(2,1)}), bf16[8,9,2048]{2,1,0:T(8,128)(2,1)}, u32[]{:S(2)}, u32[]{:S(2)}) %all-to-all-start.1) | async-done | bytes 294944 | tf_op jit(solution)/shard_map/while/body/eval_jaxpr/all_to_all | solution.py:88
  119.5 4.0 all-to-all-start
  125.3 12.4 %all-to-all-done = bf16[8,9,2048]{2,1,0:T(8,128)(2,1)S(1)} async-done(((bf16[8,9,2048]{2,1,0:T(8,128)(2,1)}), bf16[8,9,2048]{2,1,0:T(8,128)(2,1)S(1)}, u32[]{:S(2)}, u32[]{:S(2)}) %all-to-all-start) | async-done | bytes 294944 | tf_op jit(solution)/shard_map/while/body/eval_jaxpr/all_to_all | solution.py:86
  137.9 2.3 bitcast_dynamic-update-slice_fusion.11
  143.6 4.1 all-to-all-start.1
  148.0 13.8 %all-to-all-done.1 = bf16[8,9,2048]{2,1,0:T(8,128)(2,1)} async-done(((bf16[8,9,2048]{2,1,0:T(8,128)(2,1)}), bf16[8,9,2048]{2,1,0:T(8,128)(2,1)}, u32[]{:S(2)}, u32[]{:S(2)}) %all-to-all-start.1) | async-done | bytes 294944 | tf_op jit(solution)/shard_map/while/body/eval_jaxpr/all_to_all | solution.py:88
  172.1 4.0 all-to-all-start
  177.9 12.5 %all-to-all-done = bf16[8,9,2048]{2,1,0:T(8,128)(2,1)S(1)} async-done(((bf16[8,9,2048]{2,1,0:T(8,128)(2,1)}), bf16[8,9,2048]{2,1,0:T(8,128)(2,1)S(1)}, u32[]{:S(2)}, u32[]{:S(2)}) %all-to-all-start) | async-done | bytes 294944 | tf_op jit(solution)/shard_map/while/body/eval_jaxpr/all_to_all | solution.py:86
  190.5 2.3 bitcast_dynamic-update-slice_fusion.11
  196.1 4.1 all-to-all-start.1
  200.6 13.8 %all-to-all-done.1 = bf16[8,9,2048]{2,1,0:T(8,128)(2,1)} async-done(((bf16[8,9,2048]{2,1,0:T(8,128)(2,1)}), bf16[8,9,2048]{2,1,0:T(8,128)(2,1)}, u32[]{:S(2)}, u32[]{:S(2)}) %all-to-all-start.1) | async-done | bytes 294944 | tf_op jit(solution)/shard_map/while/body/eval_jaxpr/all_to_all | solution.py:88
  224.7 4.0 all-to-all-start
  230.5 12.5 %all-to-all-done = bf16[8,9,2048]{2,1,0:T(8,128)(2,1)S(1)} async-done(((bf16[8,9,2048]{2,1,0:T(8,128)(2,1)}), bf16[8,9,2048]{2,1,0:T(8,128)(2,1)S(1)}, u32[]{:S(2)}, u32[]{:S(2)}) %all-to-all-start) | async-done | bytes 294944 | tf_op jit(solution)/shard_map/while/body/eval_jaxpr/all_to_all | solution.py:86
  243.1 2.3 bitcast_dynamic-update-slice_fusion.11
  248.8 4.1 all-to-all-start.1
  253.2 13.8 %all-to-all-done.1 = bf16[8,9,2048]{2,1,0:T(8,128)(2,1)} async-done(((bf16[8,9,2048]{2,1,0:T(8,128)(2,1)}), bf16[8,9,2048]{2,1,0:T(8,128)(2,1)}, u32[]{:S(2)}, u32[]{:S(2)}) %all-to-all-start.1) | async-done | bytes 294944 | tf_op jit(solution)/shard_map/while/body/eval_jaxpr/all_to_all | solution.py:88
  272.1 4.0 all_to_all.62
  276.1 2.6 copy.40
  282.1 290.7 %while.46 = (s32[]{:T(128)}, bf16[32,2048]{1,0:T(8,128)(2,1)S(1)}, bf16[4,72,2048]{2,1,0:T(8,128)(2,1)}, bf16[4,72,640]{2,1,0:T(8,128)(2,1)}, bf16[4,72,640]{2,1...) while((s32[]{:T(128)}, bf16[32,2048]{1,0:T(8,128)(2,1)S(1)}, ...), condition=%wide.region_12.13_spmd, body=%wide.region_6.12_spmd.sunk | while | flops 597448064 | bytes 32585148 | solution.py:195
  285.8 4.0 all-to-all-start.2
  291.3 12.7 %all-to-all-done.2 = bf16[8,9,2048]{2,1,0:T(8,128)(2,1)S(1)} async-done(((bf16[8,9,2048]{2,1,0:T(8,128)(2,1)}), bf16[8,9,2048]{2,1,0:T(8,128)(2,1)S(1)}, u32[]{:S(2)}, u32[]{:S(2)}) %all-to-all-start.2) | async-done | bytes 294944 | tf_op jit(solution)/shard_map/while/body/eval_jaxpr/all_to_all | solution.py:152
  304.8 3.5 bitcast_dynamic-update-slice_fusion.12
  311.9 1.9 reshape.238
  313.8 4.1 all-to-all-start.3
  318.9 13.2 %all-to-all-done.3 = bf16[8,9,2048]{2,1,0:T(8,128)(2,1)} async-done(((bf16[8,9,2048]{2,1,0:T(8,128)(2,1)}), bf16[8,9,2048]{2,1,0:T(8,128)(2,1)}, u32[]{:S(2)}, u32[]{:S(2)}) %all-to-all-start.3) | async-done | bytes 294944 | tf_op jit(solution)/shard_map/while/body/eval_jaxpr/all_to_all | solution.py:163
  342.4 3.6 all-to-all-start.2
  347.6 14.2 %all-to-all-done.2 = bf16[8,9,2048]{2,1,0:T(8,128)(2,1)S(1)} async-done(((bf16[8,9,2048]{2,1,0:T(8,128)(2,1)}), bf16[8,9,2048]{2,1,0:T(8,128)(2,1)S(1)}, u32[]{:S(2)}, u32[]{:S(2)}) %all-to-all-start.2) | async-done | bytes 294944 | tf_op jit(solution)/shard_map/while/body/eval_jaxpr/all_to_all | solution.py:152
  362.6 3.5 bitcast_dynamic-update-slice_fusion.12
  369.7 1.9 reshape.238
  371.6 4.1 all-to-all-start.3
  376.6 13.9 %all-to-all-done.3 = bf16[8,9,2048]{2,1,0:T(8,128)(2,1)} async-done(((bf16[8,9,2048]{2,1,0:T(8,128)(2,1)}), bf16[8,9,2048]{2,1,0:T(8,128)(2,1)}, u32[]{:S(2)}, u32[]{:S(2)}) %all-to-all-start.3) | async-done | bytes 294944 | tf_op jit(solution)/shard_map/while/body/eval_jaxpr/all_to_all | solution.py:163
  400.9 3.6 all-to-all-start.2
  406.1 14.2 %all-to-all-done.2 = bf16[8,9,2048]{2,1,0:T(8,128)(2,1)S(1)} async-done(((bf16[8,9,2048]{2,1,0:T(8,128)(2,1)}), bf16[8,9,2048]{2,1,0:T(8,128)(2,1)S(1)}, u32[]{:S(2)}, u32[]{:S(2)}) %all-to-all-start.2) | async-done | bytes 294944 | tf_op jit(solution)/shard_map/while/body/eval_jaxpr/all_to_all | solution.py:152
  421.1 3.5 bitcast_dynamic-update-slice_fusion.12
  430.1 4.1 all-to-all-start.3
  435.1 13.9 %all-to-all-done.3 = bf16[8,9,2048]{2,1,0:T(8,128)(2,1)} async-done(((bf16[8,9,2048]{2,1,0:T(8,128)(2,1)}), bf16[8,9,2048]{2,1,0:T(8,128)(2,1)}, u32[]{:S(2)}, u32[]{:S(2)}) %all-to-all-start.3) | async-done | bytes 294944 | tf_op jit(solution)/shard_map/while/body/eval_jaxpr/all_to_all | solution.py:163
  459.4 3.6 all-to-all-start.2
  464.6 14.2 %all-to-all-done.2 = bf16[8,9,2048]{2,1,0:T(8,128)(2,1)S(1)} async-done(((bf16[8,9,2048]{2,1,0:T(8,128)(2,1)}), bf16[8,9,2048]{2,1,0:T(8,128)(2,1)S(1)}, u32[]{:S(2)}, u32[]{:S(2)}) %all-to-all-start.2) | async-done | bytes 294944 | tf_op jit(solution)/shard_map/while/body/eval_jaxpr/all_to_all | solution.py:152
  479.7 3.5 bitcast_dynamic-update-slice_fusion.12
  488.6 4.1 all-to-all-start.3
  493.7 13.9 %all-to-all-done.3 = bf16[8,9,2048]{2,1,0:T(8,128)(2,1)} async-done(((bf16[8,9,2048]{2,1,0:T(8,128)(2,1)}), bf16[8,9,2048]{2,1,0:T(8,128)(2,1)}, u32[]{:S(2)}, u32[]{:S(2)}) %all-to-all-start.3) | async-done | bytes 294944 | tf_op jit(solution)/shard_map/while/body/eval_jaxpr/all_to_all | solution.py:163
  518.0 3.6 all-to-all-start.2
  523.1 14.2 %all-to-all-done.2 = bf16[8,9,2048]{2,1,0:T(8,128)(2,1)S(1)} async-done(((bf16[8,9,2048]{2,1,0:T(8,128)(2,1)}), bf16[8,9,2048]{2,1,0:T(8,128)(2,1)S(1)}, u32[]{:S(2)}, u32[]{:S(2)}) %all-to-all-start.2) | async-done | bytes 294944 | tf_op jit(solution)/shard_map/while/body/eval_jaxpr/all_to_all | solution.py:152
  538.2 3.6 bitcast_dynamic-update-slice_fusion.12
  547.2 4.1 all-to-all-start.3
  552.3 13.9 %all-to-all-done.3 = bf16[8,9,2048]{2,1,0:T(8,128)(2,1)} async-done(((bf16[8,9,2048]{2,1,0:T(8,128)(2,1)}), bf16[8,9,2048]{2,1,0:T(8,128)(2,1)}, u32[]{:S(2)}, u32[]{:S(2)}) %all-to-all-start.3) | async-done | bytes 294944 | tf_op jit(solution)/shard_map/while/body/eval_jaxpr/all_to_all | solution.py:163
  572.9 4.6 all-to-all-start.4
  579.8 22.0 %all_gather.11 = bf16[576,640]{1,0:T(8,128)(2,1)S(1)} all-gather(bf16[288,640]{1,0:T(8,128)(2,1)S(1)} %bitcast.206), channel_id=1, replica_groups=mesh['section'=2,'expert'=8,'dp'=2] {'dp'}, dimensions={0}, use_global_device_ids=true | all-gather | bytes 1105920 | tf_op jit(solution)/shard_map/all_gather | solution.py:209
  601.7 11.2 %all_gather.10 = bf16[576,640]{1,0:T(8,128)(2,1)S(1)} all-gather(bf16[288,640]{1,0:T(8,128)(2,1)S(1)} %bitcast.204), channel_id=1, replica_groups=mesh['section'=2,'expert'=8,'dp'=2] {'dp'}, dimensions={0}, use_global_device_ids=true | all-gather | bytes 1105920 | tf_op jit(solution)/shard_map/all_gather | solution.py:208
  613.0 3.7 all-to-all-start.5
  616.7 22.6 %all_gather.9 = bf16[576,640]{1,0:T(8,128)(2,1)S(1)} all-gather(bf16[288,640]{1,0:T(8,128)(2,1)S(1)} %bitcast.205), channel_id=1, replica_groups=mesh['section'=2,'expert'=8,'dp'=2] {'dp'}, dimensions={0}, use_global_device_ids=true | all-gather | bytes 1105920 | tf_op jit(solution)/shard_map/all_gather | solution.py:207
  639.3 4.1 convolution_bitcast_fusion.3
  643.4 4.1 convolution_bitcast_fusion.2
  647.6 2.7 convolution_bitcast_fusion.1
  (390 shorter events, 180.3 us)
Async XLA Ops:
  2.2 3.0 copy-start
  2.2 3.0 copy-start.12
  10.4 21.8 %all-to-all-start = ((bf16[8,9,2048]{2,1,0:T(8,128)(2,1)}), bf16[8,9,2048]{2,1,0:T(8,128)(2,1)S(1)}, u32[]{:S(2)}, u32[]{:S(2)}) async-start(bf16[8,9,2048]{2,1,0:T(8,128)(2,1)} %reshape.231), calls=%async_computation | async-start | bytes 1048576 | tf_op jit(solution)/shard_map/while/body/eval_jaxpr/all_to_all | solution.py:86
  32.4 2.3 copy-start.1
  32.4 2.3 copy-start.7
  34.7 1.8 copy-start.3
  38.0 18.4 %all-to-all-start.1 = ((bf16[8,9,2048]{2,1,0:T(8,128)(2,1)}), bf16[8,9,2048]{2,1,0:T(8,128)(2,1)}, u32[]{:S(2)}, u32[]{:S(2)}) async-start(bf16[8,9,2048]{2,1,0:T(8,128)(2,1)} %reshape.233), calls=%async_computation.1 | async-start | bytes 1048576 | tf_op jit(solution)/shard_map/while/body/eval_jaxpr/all_to_all | solution.py:88
  42.4 15.9 %copy-start.5 = (bf16[32,2048]{1,0:T(8,128)(2,1)S(1)}, bf16[32,2048]{1,0:T(8,128)(2,1)}, u32[]{:S(2)}) copy-start(bf16[32,2048]{1,0:T(8,128)(2,1)} %copy-done.4) | copy-start | bytes 393220 | tf_op jit(solution)/shard_map/while
  58.4 3.1 collective-permute-start
  66.7 18.4 %all-to-all-start = ((bf16[8,9,2048]{2,1,0:T(8,128)(2,1)}), bf16[8,9,2048]{2,1,0:T(8,128)(2,1)S(1)}, u32[]{:S(2)}, u32[]{:S(2)}) async-start(bf16[8,9,2048]{2,1,0:T(8,128)(2,1)} %reshape.231), calls=%async_computation | async-start | bytes 1048576 | tf_op jit(solution)/shard_map/while/body/eval_jaxpr/all_to_all | solution.py:86
  85.3 2.3 copy-start.1
  85.3 2.3 copy-start.7
  87.6 1.8 copy-start.3
  90.9 18.3 %all-to-all-start.1 = ((bf16[8,9,2048]{2,1,0:T(8,128)(2,1)}), bf16[8,9,2048]{2,1,0:T(8,128)(2,1)}, u32[]{:S(2)}, u32[]{:S(2)}) async-start(bf16[8,9,2048]{2,1,0:T(8,128)(2,1)} %reshape.233), calls=%async_computation.1 | async-start | bytes 1048576 | tf_op jit(solution)/shard_map/while/body/eval_jaxpr/all_to_all | solution.py:88
  95.4 15.7 %copy-start.5 = (bf16[32,2048]{1,0:T(8,128)(2,1)S(1)}, bf16[32,2048]{1,0:T(8,128)(2,1)}, u32[]{:S(2)}) copy-start(bf16[32,2048]{1,0:T(8,128)(2,1)} %copy-done.4) | copy-start | bytes 393220 | tf_op jit(solution)/shard_map/while
  111.2 3.1 collective-permute-start
  119.5 18.2 %all-to-all-start = ((bf16[8,9,2048]{2,1,0:T(8,128)(2,1)}), bf16[8,9,2048]{2,1,0:T(8,128)(2,1)S(1)}, u32[]{:S(2)}, u32[]{:S(2)}) async-start(bf16[8,9,2048]{2,1,0:T(8,128)(2,1)} %reshape.231), calls=%async_computation | async-start | bytes 1048576 | tf_op jit(solution)/shard_map/while/body/eval_jaxpr/all_to_all | solution.py:86
  137.9 2.3 copy-start.1
  137.9 2.3 copy-start.7
  140.2 1.8 copy-start.3
  143.6 18.2 %all-to-all-start.1 = ((bf16[8,9,2048]{2,1,0:T(8,128)(2,1)}), bf16[8,9,2048]{2,1,0:T(8,128)(2,1)}, u32[]{:S(2)}, u32[]{:S(2)}) async-start(bf16[8,9,2048]{2,1,0:T(8,128)(2,1)} %reshape.233), calls=%async_computation.1 | async-start | bytes 1048576 | tf_op jit(solution)/shard_map/while/body/eval_jaxpr/all_to_all | solution.py:88
  148.0 15.7 %copy-start.5 = (bf16[32,2048]{1,0:T(8,128)(2,1)S(1)}, bf16[32,2048]{1,0:T(8,128)(2,1)}, u32[]{:S(2)}) copy-start(bf16[32,2048]{1,0:T(8,128)(2,1)} %copy-done.4) | copy-start | bytes 393220 | tf_op jit(solution)/shard_map/while
  163.8 3.1 collective-permute-start
  172.1 18.2 %all-to-all-start = ((bf16[8,9,2048]{2,1,0:T(8,128)(2,1)}), bf16[8,9,2048]{2,1,0:T(8,128)(2,1)S(1)}, u32[]{:S(2)}, u32[]{:S(2)}) async-start(bf16[8,9,2048]{2,1,0:T(8,128)(2,1)} %reshape.231), calls=%async_computation | async-start | bytes 1048576 | tf_op jit(solution)/shard_map/while/body/eval_jaxpr/all_to_all | solution.py:86
  190.5 2.3 copy-start.1
  190.5 2.3 copy-start.7
  192.8 1.8 copy-start.3
  196.1 18.3 %all-to-all-start.1 = ((bf16[8,9,2048]{2,1,0:T(8,128)(2,1)}), bf16[8,9,2048]{2,1,0:T(8,128)(2,1)}, u32[]{:S(2)}, u32[]{:S(2)}) async-start(bf16[8,9,2048]{2,1,0:T(8,128)(2,1)} %reshape.233), calls=%async_computation.1 | async-start | bytes 1048576 | tf_op jit(solution)/shard_map/while/body/eval_jaxpr/all_to_all | solution.py:88
  200.6 15.7 %copy-start.5 = (bf16[32,2048]{1,0:T(8,128)(2,1)S(1)}, bf16[32,2048]{1,0:T(8,128)(2,1)}, u32[]{:S(2)}) copy-start(bf16[32,2048]{1,0:T(8,128)(2,1)} %copy-done.4) | copy-start | bytes 393220 | tf_op jit(solution)/shard_map/while
  216.4 3.1 collective-permute-start
  224.7 18.2 %all-to-all-start = ((bf16[8,9,2048]{2,1,0:T(8,128)(2,1)}), bf16[8,9,2048]{2,1,0:T(8,128)(2,1)S(1)}, u32[]{:S(2)}, u32[]{:S(2)}) async-start(bf16[8,9,2048]{2,1,0:T(8,128)(2,1)} %reshape.231), calls=%async_computation | async-start | bytes 1048576 | tf_op jit(solution)/shard_map/while/body/eval_jaxpr/all_to_all | solution.py:86
  243.1 2.3 copy-start.1
  243.1 2.3 copy-start.7
  245.4 1.8 copy-start.3
  248.8 18.3 %all-to-all-start.1 = ((bf16[8,9,2048]{2,1,0:T(8,128)(2,1)}), bf16[8,9,2048]{2,1,0:T(8,128)(2,1)}, u32[]{:S(2)}, u32[]{:S(2)}) async-start(bf16[8,9,2048]{2,1,0:T(8,128)(2,1)} %reshape.233), calls=%async_computation.1 | async-start | bytes 1048576 | tf_op jit(solution)/shard_map/while/body/eval_jaxpr/all_to_all | solution.py:88
  253.2 15.7 %copy-start.5 = (bf16[32,2048]{1,0:T(8,128)(2,1)S(1)}, bf16[32,2048]{1,0:T(8,128)(2,1)}, u32[]{:S(2)}) copy-start(bf16[32,2048]{1,0:T(8,128)(2,1)} %copy-done.4) | copy-start | bytes 393220 | tf_op jit(solution)/shard_map/while
  269.0 3.1 collective-permute-start
  285.8 18.2 %all-to-all-start.2 = ((bf16[8,9,2048]{2,1,0:T(8,128)(2,1)}), bf16[8,9,2048]{2,1,0:T(8,128)(2,1)S(1)}, u32[]{:S(2)}, u32[]{:S(2)}) async-start(bf16[8,9,2048]{2,1,0:T(8,128)(2,1)} %reshape.236), calls=%async_computation.2 | async-start | bytes 1048576 | tf_op jit(solution)/shard_map/while/body/eval_jaxpr/all_to_all | solution.py:152
  308.4 1.7 copy-start.2
  313.8 18.2 %all-to-all-start.3 = ((bf16[8,9,2048]{2,1,0:T(8,128)(2,1)}), bf16[8,9,2048]{2,1,0:T(8,128)(2,1)}, u32[]{:S(2)}, u32[]{:S(2)}) async-start(bf16[8,9,2048]{2,1,0:T(8,128)(2,1)} %reshape.238), calls=%async_computation.3 | async-start | bytes 1048576 | tf_op jit(solution)/shard_map/while/body/eval_jaxpr/all_to_all | solution.py:163
  318.9 17.9 %copy-start.6 = (bf16[1,72,2048]{2,1,0:T(8,128)(2,1)S(1)}, bf16[1,72,2048]{2,1,0:T(8,128)(2,1)}, u32[]{:S(2)}) copy-start(bf16[1,72,2048]{2,1,0:T(8,128)(2,1)} %reshape.240) | copy-start | bytes 884740 | tf_op jit(solution)/shard_map/while
  335.5 3.2 collective-permute-start.1
  342.4 19.4 %all-to-all-start.2 = ((bf16[8,9,2048]{2,1,0:T(8,128)(2,1)}), bf16[8,9,2048]{2,1,0:T(8,128)(2,1)S(1)}, u32[]{:S(2)}, u32[]{:S(2)}) async-start(bf16[8,9,2048]{2,1,0:T(8,128)(2,1)} %reshape.236), calls=%async_computation.2 | async-start | bytes 1048576 | tf_op jit(solution)/shard_map/while/body/eval_jaxpr/all_to_all | solution.py:152
  366.2 1.7 copy-start.2
  371.6 18.9 %all-to-all-start.3 = ((bf16[8,9,2048]{2,1,0:T(8,128)(2,1)}), bf16[8,9,2048]{2,1,0:T(8,128)(2,1)}, u32[]{:S(2)}, u32[]{:S(2)}) async-start(bf16[8,9,2048]{2,1,0:T(8,128)(2,1)} %reshape.238), calls=%async_computation.3 | async-start | bytes 1048576 | tf_op jit(solution)/shard_map/while/body/eval_jaxpr/all_to_all | solution.py:163
  376.6 18.6 %copy-start.6 = (bf16[1,72,2048]{2,1,0:T(8,128)(2,1)S(1)}, bf16[1,72,2048]{2,1,0:T(8,128)(2,1)}, u32[]{:S(2)}) copy-start(bf16[1,72,2048]{2,1,0:T(8,128)(2,1)} %reshape.240) | copy-start | bytes 884740 | tf_op jit(solution)/shard_map/while
  394.0 3.2 collective-permute-start.1
  400.9 19.4 %all-to-all-start.2 = ((bf16[8,9,2048]{2,1,0:T(8,128)(2,1)}), bf16[8,9,2048]{2,1,0:T(8,128)(2,1)S(1)}, u32[]{:S(2)}, u32[]{:S(2)}) async-start(bf16[8,9,2048]{2,1,0:T(8,128)(2,1)} %reshape.236), calls=%async_computation.2 | async-start | bytes 1048576 | tf_op jit(solution)/shard_map/while/body/eval_jaxpr/all_to_all | solution.py:152
  430.1 19.0 %all-to-all-start.3 = ((bf16[8,9,2048]{2,1,0:T(8,128)(2,1)}), bf16[8,9,2048]{2,1,0:T(8,128)(2,1)}, u32[]{:S(2)}, u32[]{:S(2)}) async-start(bf16[8,9,2048]{2,1,0:T(8,128)(2,1)} %reshape.238), calls=%async_computation.3 | async-start | bytes 1048576 | tf_op jit(solution)/shard_map/while/body/eval_jaxpr/all_to_all | solution.py:163
  435.1 18.7 %copy-start.6 = (bf16[1,72,2048]{2,1,0:T(8,128)(2,1)S(1)}, bf16[1,72,2048]{2,1,0:T(8,128)(2,1)}, u32[]{:S(2)}) copy-start(bf16[1,72,2048]{2,1,0:T(8,128)(2,1)} %reshape.240) | copy-start | bytes 884740 | tf_op jit(solution)/shard_map/while
  452.5 3.2 collective-permute-start.1
  459.4 19.4 %all-to-all-start.2 = ((bf16[8,9,2048]{2,1,0:T(8,128)(2,1)}), bf16[8,9,2048]{2,1,0:T(8,128)(2,1)S(1)}, u32[]{:S(2)}, u32[]{:S(2)}) async-start(bf16[8,9,2048]{2,1,0:T(8,128)(2,1)} %reshape.236), calls=%async_computation.2 | async-start | bytes 1048576 | tf_op jit(solution)/shard_map/while/body/eval_jaxpr/all_to_all | solution.py:152
  488.6 19.0 %all-to-all-start.3 = ((bf16[8,9,2048]{2,1,0:T(8,128)(2,1)}), bf16[8,9,2048]{2,1,0:T(8,128)(2,1)}, u32[]{:S(2)}, u32[]{:S(2)}) async-start(bf16[8,9,2048]{2,1,0:T(8,128)(2,1)} %reshape.238), calls=%async_computation.3 | async-start | bytes 1048576 | tf_op jit(solution)/shard_map/while/body/eval_jaxpr/all_to_all | solution.py:163
  493.7 18.7 %copy-start.6 = (bf16[1,72,2048]{2,1,0:T(8,128)(2,1)S(1)}, bf16[1,72,2048]{2,1,0:T(8,128)(2,1)}, u32[]{:S(2)}) copy-start(bf16[1,72,2048]{2,1,0:T(8,128)(2,1)} %reshape.240) | copy-start | bytes 884740 | tf_op jit(solution)/shard_map/while
  511.1 3.2 collective-permute-start.1
  518.0 19.4 %all-to-all-start.2 = ((bf16[8,9,2048]{2,1,0:T(8,128)(2,1)}), bf16[8,9,2048]{2,1,0:T(8,128)(2,1)S(1)}, u32[]{:S(2)}, u32[]{:S(2)}) async-start(bf16[8,9,2048]{2,1,0:T(8,128)(2,1)} %reshape.236), calls=%async_computation.2 | async-start | bytes 1048576 | tf_op jit(solution)/shard_map/while/body/eval_jaxpr/all_to_all | solution.py:152
  547.2 19.0 %all-to-all-start.3 = ((bf16[8,9,2048]{2,1,0:T(8,128)(2,1)}), bf16[8,9,2048]{2,1,0:T(8,128)(2,1)}, u32[]{:S(2)}, u32[]{:S(2)}) async-start(bf16[8,9,2048]{2,1,0:T(8,128)(2,1)} %reshape.238), calls=%async_computation.3 | async-start | bytes 1048576 | tf_op jit(solution)/shard_map/while/body/eval_jaxpr/all_to_all | solution.py:163
  552.3 18.7 %copy-start.6 = (bf16[1,72,2048]{2,1,0:T(8,128)(2,1)S(1)}, bf16[1,72,2048]{2,1,0:T(8,128)(2,1)}, u32[]{:S(2)}) copy-start(bf16[1,72,2048]{2,1,0:T(8,128)(2,1)} %reshape.240) | copy-start | bytes 884740 | tf_op jit(solution)/shard_map/while
  569.6 3.2 collective-permute-start.1
  572.9 4.6 copy-start.8
  572.9 40.1 %all-to-all-start.4 = ((bf16[288,2,1024]{2,0,1:T(8,128)(2,1)}), bf16[288,2,1024]{2,0,1:T(8,128)(2,1)}, u32[]{:S(2)}, u32[]{:S(2)}) async-start(bf16[288,2,1024]{2,0,1:T(8,128)(2,1)} %copy.40), calls=%async_computation.4 | async-start | bytes 2359296 | tf_op jit(solution)/shard_map/all_to_all | solution.py:203
  578.4 23.4 %copy-start.9 = (bf16[4,72,640]{2,1,0:T(8,128)(2,1)S(1)}, bf16[4,72,640]{2,1,0:T(8,128)(2,1)}, u32[]{:S(2)}) copy-start(bf16[4,72,640]{2,1,0:T(8,128)(2,1)} %get-tuple-element.649) | copy-start | bytes 1105924
  613.0 3.8 copy-start.10
  613.0 34.6 %all-to-all-start.5 = ((bf16[288,2,1024]{2,0,1:T(8,128)(2,1)}), bf16[288,2,1024]{2,0,1:T(8,128)(2,1)S(1)}, u32[]{:S(2)}, u32[]{:S(2)}) async-start(bf16[288,2,1024]{2,0,1:T(8,128)(2,1)} %copy.41), calls=%async_computation.5 | async-start | bytes 2359296 | tf_op jit(solution)/shard_map/all_to_all | solution.py:204
  (9 other events, 9.9 us)
where the time goes:
time: 655 us; the launch traced here: 650 us
  waiting for transfers between devices  271 us (41%)
  starting transfers between devices  105 us (16%)
  local copies, waits for them, and re-layouts  99 us (15%)
  matrix products  76.2 us (12%)
  blocking collectives  55.8 us (9%)
  other arithmetic  41.8 us (6%)
    all_to_all x5, waiting for transfers between devices, backward_step(): lax.all_to_all(outgoing.reshape(experts, cap_slots, model_width), 'expert...  69.5 us
    all_to_all x5, waiting for transfers between devices, forward_step(): lax.all_to_all(produced, 'expert', split_axis=0, concat_axis=0, tiled=True)  69.3 us
    all_to_all x5, waiting for transfers between devices, backward_step(): lax.all_to_all(d_rows.reshape(experts, cap_slots, model_width), 'expert',...  68.8 us
    all_to_all x5, waiting for transfers between devices, forward_step(): lax.all_to_all(outgoing, 'expert', split_axis=0, concat_axis=0, tiled=True)  62.5 us
    dynamic_update_slice x15, other arithmetic, keep_entry(): lax.dynamic_update_index_in_dim(store, jnp.where(is_live, value, previous...  25.6 us
    all_to_all x5, starting transfers between devices, forward_step(): lax.all_to_all(outgoing, 'expert', split_axis=0, concat_axis=0, tiled=True)  23.4 us
    all_gather x1, blocking collectives, shards(): lax.all_gather(dgate_all, 'dp', axis=0, tiled=True)  22.6 us
    all_gather x1, blocking collectives, shards(): lax.all_gather(act_all, 'dp', axis=0, tiled=True)  22 us
  transfers between devices with their start and end apart: 32, of which 25 were waited for; matrix products, arithmetic and copies ran while one was open for 8% of the time, Pallas kernels for 0%

commit v1 on v0

--- a/solution.py
+++ b/solution.py
@@ -6,6 +6,29 @@
 epsilon = 1e-05
 contract_rows = (((0,), (0,)), ((), ()))
 contract_cols = (((1,), (1,)), ((), ()))
+
+
+def split_up(shard, dim, size):
+    before, after = (shard.shape[:dim], shard.shape[dim + 1 :])
+    return jnp.moveaxis(shard.reshape(*before, size, -1, *after), dim, 0)
+
+
+def joined_along(tiles, dim):
+    tiles = jnp.moveaxis(tiles, 0, dim)
+    lengths = tiles.shape
+    return tiles.reshape(*lengths[:dim], lengths[dim] * lengths[dim + 1], *lengths[dim + 2 :])
+
+
+def exchange_directly(x, axis, split_dim, concat_dim):
+    size, here = (lax.axis_size(axis), lax.axis_index(axis))
+    tiles = split_up(x, split_dim, size)
+    out = tiles
+    for lap in range(1, size):
+        target, source = ((here + lap) % size, (here - lap) % size)
+        sent = lax.dynamic_index_in_dim(tiles, target, 0)
+        partner_block = lax.ppermute(sent, axis, [(i, (i + lap) % size) for i in range(size)])
+        out = lax.dynamic_update_slice_in_dim(out, partner_block, source, axis=0)
+    return joined_along(out, concat_dim)
 
 
 def shifted(value, axis, by):
@@ -83,7 +106,7 @@
         ).astype(jnp.bfloat16)
         outgoing = outgoing.reshape(experts, cap_slots, model_width)
         received, pre_gate, pre_up, produced = expert_forward(
-            lax.all_to_all(outgoing, "expert", split_axis=0, concat_axis=0, tiled=True)
+            exchange_directly(outgoing, "expert", 0, 0)
         )
         returned = lax.all_to_all(produced, "expert", split_axis=0, concat_axis=0, tiled=True)
         chosen = jnp.einsum(

time: 655 us -> 666 us (1.017)
  starting transfers between devices: 105 us -> 134 us
  waiting for transfers between devices: 271 us -> 248 us
    all_to_all x5 -> x0, waiting for transfers between devices: 62.5 us -> none  [forward_step(): lax.all_to_all(outgoing, 'expert', split_axis=0, concat_axis=0, tiled=True)]
    ppermute x0 -> x35, starting transfers between devices: none -> 50.1 us  [exchange_directly(): lax.ppermute(sent, axis, [(i, (i + lap) % size) for i in range(size)])]
    ppermute x0 -> x35, waiting for transfers between devices: none -> 46.1 us  [exchange_directly(): lax.ppermute(sent, axis, [(i, (i + lap) % size) for i in range(size)])]
    all_to_all x5 -> x0, starting transfers between devices: 23.4 us -> none  [forward_step(): lax.all_to_all(outgoing, 'expert', split_axis=0, concat_axis=0, tiled=True)]
    dynamic_slice x0 -> x10, local copies, waits for them, and re-layouts: none -> 7.51 us  [exchange_directly(): sent = lax.dynamic_index_in_dim(tiles, target, 0)]
  transfers between devices with their start and end apart: 32 -> 62, of which waited for: 25 -> 40; matrix products, arithmetic and copies ran while one was open for 8% -> 8% of each run, Pallas kernels for 0% -> 0%
where the time goes in v1:
time: 666 us; the launch traced here: 662 us
  waiting for transfers between devices  248 us (37%)
  starting transfers between devices  134 us (20%)
  local copies, waits for them, and re-layouts  103 us (15%)
  matrix products  76.4 us (11%)
  blocking collectives  55.8 us (8%)
  other arithmetic  41.9 us (6%)
    all_to_all x5, waiting for transfers between devices, backward_step(): lax.all_to_all(outgoing.reshape(experts, cap_slots, model_width), 'expert...  69.6 us
    all_to_all x5, waiting for transfers between devices, backward_step(): lax.all_to_all(d_rows.reshape(experts, cap_slots, model_width), 'expert',...  68.8 us
    all_to_all x5, waiting for transfers between devices, forward_step(): lax.all_to_all(produced, 'expert', split_axis=0, concat_axis=0, tiled=True)  63.2 us
    ppermute x35, starting transfers between devices, exchange_directly(): lax.ppermute(sent, axis, [(i, (i + lap) % size) for i in range(size)])  50.1 us
    ppermute x35, waiting for transfers between devices, exchange_directly(): lax.ppermute(sent, axis, [(i, (i + lap) % size) for i in range(size)])  46.1 us
    dynamic_update_slice x15, other arithmetic, keep_entry(): lax.dynamic_update_index_in_dim(store, jnp.where(is_live, value, previous...  25.6 us
    all_to_all x5, starting transfers between devices, forward_step(): lax.all_to_all(produced, 'expert', split_axis=0, concat_axis=0, tiled=True)  24.1 us
    all_gather x1, blocking collectives, shards(): lax.all_gather(dgate_all, 'dp', axis=0, tiled=True)  22.6 us
  transfers between devices with their start and end apart: 62, of which 40 were waited for; matrix products, arithmetic and copies ran while one was open for 8% of the time, Pallas kernels for 0%

profile of v1, /device:TPU:0, one launch (start us, length us, event | category | flops | bytes accessed | tf_op | source)
XLA Modules:
  0.0 662.0 jit_solution(927160713500338190)
XLA Ops:
  5.2 278.4 %while.46 = (s32[]{:T(128)}, bf16[32,2048]{1,0:T(8,128)(2,1)S(1)}, bf16[4,32,2048]{2,1,0:T(8,128)(2,1)}, bf16[4,72,2048]{2,1,0:T(8,128)(2,1)}, f32[4,72,640]{2,1...) while((s32[]{:T(128)}, bf16[32,2048]{1,0:T(8,128)(2,1)S(1)}, ...), condition=%wide.region_5.6_spmd, body=%wide.region_0.5_spmd.sunk | while | flops 596246080 | bytes 45279384 | solution.py:135
  9.7 3.0 collective-permute-start
  12.7 5.4 collective-permute-done
  24.2 3.6 collective-permute-start.4
  39.2 5.4 all-to-all-start
  44.9 13.3 %all-to-all-done = bf16[8,9,2048]{2,1,0:T(8,128)(2,1)} async-done(((bf16[8,9,2048]{2,1,0:T(8,128)(2,1)}), bf16[8,9,2048]{2,1,0:T(8,128)(2,1)}, u32[]{:S(2)}, u32[]{:S(2)}) %all-to-all-start) | async-done | bytes 294944 | tf_op jit(solution)/shard_map/while/body/eval_jaxpr/all_to_all | solution.py:111
  69.3 5.6 collective-permute-done
  78.2 2.6 collective-permute-start.3
  82.0 3.8 collective-permute-start.5
  95.9 4.7 all-to-all-start
  100.8 12.5 %all-to-all-done = bf16[8,9,2048]{2,1,0:T(8,128)(2,1)} async-done(((bf16[8,9,2048]{2,1,0:T(8,128)(2,1)}), bf16[8,9,2048]{2,1,0:T(8,128)(2,1)}, u32[]{:S(2)}, u32[]{:S(2)}) %all-to-all-start) | async-done | bytes 294944 | tf_op jit(solution)/shard_map/while/body/eval_jaxpr/all_to_all | solution.py:111
  124.4 5.6 collective-permute-done
  133.3 2.6 collective-permute-start.3
  137.1 3.8 collective-permute-start.5
  151.0 4.7 all-to-all-start
  155.9 12.4 %all-to-all-done = bf16[8,9,2048]{2,1,0:T(8,128)(2,1)} async-done(((bf16[8,9,2048]{2,1,0:T(8,128)(2,1)}), bf16[8,9,2048]{2,1,0:T(8,128)(2,1)}, u32[]{:S(2)}, u32[]{:S(2)}) %all-to-all-start) | async-done | bytes 294944 | tf_op jit(solution)/shard_map/while/body/eval_jaxpr/all_to_all | solution.py:111
  179.4 5.6 collective-permute-done
  188.3 2.5 collective-permute-start.3
  192.2 3.8 collective-permute-start.5
  200.4 2.3 bitcast_dynamic-update-slice_fusion.11
  206.1 4.7 all-to-all-start
  211.0 12.4 %all-to-all-done = bf16[8,9,2048]{2,1,0:T(8,128)(2,1)} async-done(((bf16[8,9,2048]{2,1,0:T(8,128)(2,1)}), bf16[8,9,2048]{2,1,0:T(8,128)(2,1)}, u32[]{:S(2)}, u32[]{:S(2)}) %all-to-all-start) | async-done | bytes 294944 | tf_op jit(solution)/shard_map/while/body/eval_jaxpr/all_to_all | solution.py:111
  234.5 5.6 collective-permute-done
  243.4 2.6 collective-permute-start.3
  247.2 3.8 collective-permute-start.5
  255.5 2.3 bitcast_dynamic-update-slice_fusion.11
  261.1 4.7 all-to-all-start
  266.1 12.4 %all-to-all-done = bf16[8,9,2048]{2,1,0:T(8,128)(2,1)} async-done(((bf16[8,9,2048]{2,1,0:T(8,128)(2,1)}), bf16[8,9,2048]{2,1,0:T(8,128)(2,1)}, u32[]{:S(2)}, u32[]{:S(2)}) %all-to-all-start) | async-done | bytes 294944 | tf_op jit(solution)/shard_map/while/body/eval_jaxpr/all_to_all | solution.py:111
  283.6 4.0 all_to_all.56
  287.6 2.6 copy.40
  293.6 290.9 %while.47 = (s32[]{:T(128)}, bf16[32,2048]{1,0:T(8,128)(2,1)S(1)}, bf16[4,72,2048]{2,1,0:T(8,128)(2,1)}, bf16[4,72,640]{2,1,0:T(8,128)(2,1)}, bf16[4,72,640]{2,1...) while((s32[]{:T(128)}, bf16[32,2048]{1,0:T(8,128)(2,1)S(1)}, ...), condition=%wide.region_12.13_spmd, body=%wide.region_6.12_spmd.sunk | while | flops 597448064 | bytes 32585148 | solution.py:218
  297.3 3.6 all-to-all-start.1
  302.5 12.7 %all-to-all-done.1 = bf16[8,9,2048]{2,1,0:T(8,128)(2,1)S(1)} async-done(((bf16[8,9,2048]{2,1,0:T(8,128)(2,1)}), bf16[8,9,2048]{2,1,0:T(8,128)(2,1)S(1)}, u32[]{:S(2)}, u32[]{:S(2)}) %all-to-all-start.1) | async-done | bytes 294944 | tf_op jit(solution)/shard_map/while/body/eval_jaxpr/all_to_all | solution.py:175
  316.1 3.5 bitcast_dynamic-update-slice_fusion.12
  325.1 4.1 all-to-all-start.2
  330.2 13.2 %all-to-all-done.2 = bf16[8,9,2048]{2,1,0:T(8,128)(2,1)} async-done(((bf16[8,9,2048]{2,1,0:T(8,128)(2,1)}), bf16[8,9,2048]{2,1,0:T(8,128)(2,1)}, u32[]{:S(2)}, u32[]{:S(2)}) %all-to-all-start.2) | async-done | bytes 294944 | tf_op jit(solution)/shard_map/while/body/eval_jaxpr/all_to_all | solution.py:186
  353.7 3.6 all-to-all-start.1
  359.0 14.2 %all-to-all-done.1 = bf16[8,9,2048]{2,1,0:T(8,128)(2,1)S(1)} async-done(((bf16[8,9,2048]{2,1,0:T(8,128)(2,1)}), bf16[8,9,2048]{2,1,0:T(8,128)(2,1)S(1)}, u32[]{:S(2)}, u32[]{:S(2)}) %all-to-all-start.1) | async-done | bytes 294944 | tf_op jit(solution)/shard_map/while/body/eval_jaxpr/all_to_all | solution.py:175
  374.0 3.5 bitcast_dynamic-update-slice_fusion.12
  383.0 4.1 all-to-all-start.2
  388.1 13.9 %all-to-all-done.2 = bf16[8,9,2048]{2,1,0:T(8,128)(2,1)} async-done(((bf16[8,9,2048]{2,1,0:T(8,128)(2,1)}), bf16[8,9,2048]{2,1,0:T(8,128)(2,1)}, u32[]{:S(2)}, u32[]{:S(2)}) %all-to-all-start.2) | async-done | bytes 294944 | tf_op jit(solution)/shard_map/while/body/eval_jaxpr/all_to_all | solution.py:186
  412.3 3.6 all-to-all-start.1
  417.5 14.2 %all-to-all-done.1 = bf16[8,9,2048]{2,1,0:T(8,128)(2,1)S(1)} async-done(((bf16[8,9,2048]{2,1,0:T(8,128)(2,1)}), bf16[8,9,2048]{2,1,0:T(8,128)(2,1)S(1)}, u32[]{:S(2)}, u32[]{:S(2)}) %all-to-all-start.1) | async-done | bytes 294944 | tf_op jit(solution)/shard_map/while/body/eval_jaxpr/all_to_all | solution.py:175
  432.6 3.5 bitcast_dynamic-update-slice_fusion.12
  441.6 4.1 all-to-all-start.2
  446.7 13.9 %all-to-all-done.2 = bf16[8,9,2048]{2,1,0:T(8,128)(2,1)} async-done(((bf16[8,9,2048]{2,1,0:T(8,128)(2,1)}), bf16[8,9,2048]{2,1,0:T(8,128)(2,1)}, u32[]{:S(2)}, u32[]{:S(2)}) %all-to-all-start.2) | async-done | bytes 294944 | tf_op jit(solution)/shard_map/while/body/eval_jaxpr/all_to_all | solution.py:186
  471.0 3.6 all-to-all-start.1
  476.2 14.2 %all-to-all-done.1 = bf16[8,9,2048]{2,1,0:T(8,128)(2,1)S(1)} async-done(((bf16[8,9,2048]{2,1,0:T(8,128)(2,1)}), bf16[8,9,2048]{2,1,0:T(8,128)(2,1)S(1)}, u32[]{:S(2)}, u32[]{:S(2)}) %all-to-all-start.1) | async-done | bytes 294944 | tf_op jit(solution)/shard_map/while/body/eval_jaxpr/all_to_all | solution.py:175
  491.3 3.5 bitcast_dynamic-update-slice_fusion.12
  500.3 4.1 all-to-all-start.2
  505.3 13.9 %all-to-all-done.2 = bf16[8,9,2048]{2,1,0:T(8,128)(2,1)} async-done(((bf16[8,9,2048]{2,1,0:T(8,128)(2,1)}), bf16[8,9,2048]{2,1,0:T(8,128)(2,1)}, u32[]{:S(2)}, u32[]{:S(2)}) %all-to-all-start.2) | async-done | bytes 294944 | tf_op jit(solution)/shard_map/while/body/eval_jaxpr/all_to_all | solution.py:186
  529.6 3.6 all-to-all-start.1
  534.8 14.2 %all-to-all-done.1 = bf16[8,9,2048]{2,1,0:T(8,128)(2,1)S(1)} async-done(((bf16[8,9,2048]{2,1,0:T(8,128)(2,1)}), bf16[8,9,2048]{2,1,0:T(8,128)(2,1)S(1)}, u32[]{:S(2)}, u32[]{:S(2)}) %all-to-all-start.1) | async-done | bytes 294944 | tf_op jit(solution)/shard_map/while/body/eval_jaxpr/all_to_all | solution.py:175
  549.9 3.5 bitcast_dynamic-update-slice_fusion.12
  558.9 4.1 all-to-all-start.2
  564.0 13.9 %all-to-all-done.2 = bf16[8,9,2048]{2,1,0:T(8,128)(2,1)} async-done(((bf16[8,9,2048]{2,1,0:T(8,128)(2,1)}), bf16[8,9,2048]{2,1,0:T(8,128)(2,1)}, u32[]{:S(2)}, u32[]{:S(2)}) %all-to-all-start.2) | async-done | bytes 294944 | tf_op jit(solution)/shard_map/while/body/eval_jaxpr/all_to_all | solution.py:186
  584.5 4.6 all-to-all-start.3
  591.4 22.0 %all_gather.11 = bf16[576,640]{1,0:T(8,128)(2,1)S(1)} all-gather(bf16[288,640]{1,0:T(8,128)(2,1)S(1)} %bitcast.210), channel_id=1, replica_groups=mesh['section'=2,'expert'=8,'dp'=2] {'dp'}, dimensions={0}, use_global_device_ids=true | all-gather | bytes 1105920 | tf_op jit(solution)/shard_map/all_gather | solution.py:232
  613.4 11.2 %all_gather.10 = bf16[576,640]{1,0:T(8,128)(2,1)S(1)} all-gather(bf16[288,640]{1,0:T(8,128)(2,1)S(1)} %bitcast.208), channel_id=1, replica_groups=mesh['section'=2,'expert'=8,'dp'=2] {'dp'}, dimensions={0}, use_global_device_ids=true | all-gather | bytes 1105920 | tf_op jit(solution)/shard_map/all_gather | solution.py:231
  624.7 3.7 all-to-all-start.4
  628.4 22.6 %all_gather.9 = bf16[576,640]{1,0:T(8,128)(2,1)S(1)} all-gather(bf16[288,640]{1,0:T(8,128)(2,1)S(1)} %bitcast.209), channel_id=1, replica_groups=mesh['section'=2,'expert'=8,'dp'=2] {'dp'}, dimensions={0}, use_global_device_ids=true | all-gather | bytes 1105920 | tf_op jit(solution)/shard_map/all_gather | solution.py:230
  651.0 4.1 convolution_bitcast_fusion.3
  655.1 4.1 convolution_bitcast_fusion.2
  659.2 2.7 convolution_bitcast_fusion.1
  (490 shorter events, 231.3 us)
Async XLA Ops:
  9.7 8.4 %collective-permute-start = (bf16[1,1,9,2048]{3,2,0,1:T(8,128)(2,1)S(1)}, bf16[1,1,9,2048]{3,2,0,1:T(8,128)(2,1)}, u32[]{:S(2)}, u32[]{:S(2)}) collective-permute-start(bf16[1,1,9,2048]{3,2,0,1:T(8,128)(2,1)S(1)} %constant_dynamic-slice_fusion.26), channel_id=1, source_target_pairs={{0,2},{2,4},{4,6},{6,8},{8,10},{10,12},{12,14},{14,0},{1,3},{3,5},... | collective-permute-start | bytes 110600 | tf_op jit(solution)/shard_map/while/body/eval_jaxpr/ppermute | solution.py:29
  19.6 9.5 %collective-permute-start.1 = (bf16[1,1,9,2048]{3,2,0,1:T(8,128)(2,1)}, bf16[1,1,9,2048]{3,2,0,1:T(8,128)(2,1)S(1)}, u32[]{:S(2)}, u32[]{:S(2)}) collective-permute-start(bf16[1,1,9,2048]{3,2,0,1:T(8,128)(2,1)} %get-tuple-element.995), channel_id=1, source_target_pairs={{0,4},{2,6},{4,8},{6,10},{8,12},{10,14},{12,0},{14,2},{1,5},{3,7},... | collective-permute-start | bytes 110600 | tf_op jit(solution)/shard_map/while/body/eval_jaxpr/ppermute | solution.py:29
  21.4 8.2 %collective-permute-start.2 = (bf16[1,1,9,2048]{3,2,0,1:T(8,128)(2,1)S(1)}, bf16[1,1,9,2048]{3,2,0,1:T(8,128)(2,1)S(1)}, u32[]{:S(2)}, u32[]{:S(2)}) collective-permute-start(bf16[1,1,9,2048]{3,2,0,1:T(8,128)(2,1)S(1)} %get-tuple-element.996), channel_id=1, source_target_pairs={{0,6},{2,8},{4,10},{6,12},{8,14},{10,0},{12,2},{14,4},{1,7},{3,9},... | collective-permute-start | bytes 110600 | tf_op jit(solution)/shard_map/while/body/eval_jaxpr/ppermute | solution.py:29
  22.9 7.6 %collective-permute-start.3 = (bf16[1,1,9,2048]{3,2,0,1:T(8,128)(2,1)S(1)}, bf16[1,1,9,2048]{3,2,0,1:T(8,128)(2,1)S(1)}, u32[]{:S(2)}, u32[]{:S(2)}) collective-permute-start(bf16[1,1,9,2048]{3,2,0,1:T(8,128)(2,1)S(1)} %get-tuple-element.997), channel_id=1, source_target_pairs={{0,8},{2,10},{4,12},{6,14},{8,0},{10,2},{12,4},{14,6},{1,9},{3,11}... | collective-permute-start | bytes 110600 | tf_op jit(solution)/shard_map/while/body/eval_jaxpr/ppermute | solution.py:29
  24.2 6.4 collective-permute-start.4
  27.7 5.0 collective-permute-start.5
  29.1 4.3 collective-permute-start.6
  39.2 19.0 %all-to-all-start = ((bf16[8,9,2048]{2,1,0:T(8,128)(2,1)}), bf16[8,9,2048]{2,1,0:T(8,128)(2,1)}, u32[]{:S(2)}, u32[]{:S(2)}) async-start(bf16[8,9,2048]{2,1,0:T(8,128)(2,1)} %reshape.247), calls=%async_computation | async-start | bytes 1048576 | tf_op jit(solution)/shard_map/while/body/eval_jaxpr/all_to_all | solution.py:111
  60.2 3.1 collective-permute-start.7
  67.8 7.1 %collective-permute-start = (bf16[1,1,9,2048]{3,2,0,1:T(8,128)(2,1)S(1)}, bf16[1,1,9,2048]{3,2,0,1:T(8,128)(2,1)}, u32[]{:S(2)}, u32[]{:S(2)}) collective-permute-start(bf16[1,1,9,2048]{3,2,0,1:T(8,128)(2,1)S(1)} %constant_dynamic-slice_fusion.26), channel_id=1, source_target_pairs={{0,2},{2,4},{4,6},{6,8},{8,10},{10,12},{12,14},{14,0},{1,3},{3,5},... | collective-permute-start | bytes 110600 | tf_op jit(solution)/shard_map/while/body/eval_jaxpr/ppermute | solution.py:29
  76.4 9.4 %collective-permute-start.1 = (bf16[1,1,9,2048]{3,2,0,1:T(8,128)(2,1)}, bf16[1,1,9,2048]{3,2,0,1:T(8,128)(2,1)S(1)}, u32[]{:S(2)}, u32[]{:S(2)}) collective-permute-start(bf16[1,1,9,2048]{3,2,0,1:T(8,128)(2,1)} %get-tuple-element.995), channel_id=1, source_target_pairs={{0,4},{2,6},{4,8},{6,10},{8,12},{10,14},{12,0},{14,2},{1,5},{3,7},... | collective-permute-start | bytes 110600 | tf_op jit(solution)/shard_map/while/body/eval_jaxpr/ppermute | solution.py:29
  78.2 8.2 %collective-permute-start.2 = (bf16[1,1,9,2048]{3,2,0,1:T(8,128)(2,1)S(1)}, bf16[1,1,9,2048]{3,2,0,1:T(8,128)(2,1)S(1)}, u32[]{:S(2)}, u32[]{:S(2)}) collective-permute-start(bf16[1,1,9,2048]{3,2,0,1:T(8,128)(2,1)S(1)} %get-tuple-element.996), channel_id=1, source_target_pairs={{0,6},{2,8},{4,10},{6,12},{8,14},{10,0},{12,2},{14,4},{1,7},{3,9},... | collective-permute-start | bytes 110600 | tf_op jit(solution)/shard_map/while/body/eval_jaxpr/ppermute | solution.py:29
  78.2 8.3 %collective-permute-start.3 = (bf16[1,1,9,2048]{3,2,0,1:T(8,128)(2,1)S(1)}, bf16[1,1,9,2048]{3,2,0,1:T(8,128)(2,1)S(1)}, u32[]{:S(2)}, u32[]{:S(2)}) collective-permute-start(bf16[1,1,9,2048]{3,2,0,1:T(8,128)(2,1)S(1)} %get-tuple-element.997), channel_id=1, source_target_pairs={{0,8},{2,10},{4,12},{6,14},{8,0},{10,2},{12,4},{14,6},{1,9},{3,11}... | collective-permute-start | bytes 110600 | tf_op jit(solution)/shard_map/while/body/eval_jaxpr/ppermute | solution.py:29
  80.7 5.9 collective-permute-start.4
  82.0 6.8 %collective-permute-start.5 = (bf16[1,1,9,2048]{3,2,0,1:T(8,128)(2,1)S(1)}, bf16[1,1,9,2048]{3,2,0,1:T(8,128)(2,1)S(1)}, u32[]{:S(2)}, u32[]{:S(2)}) collective-permute-start(bf16[1,1,9,2048]{3,2,0,1:T(8,128)(2,1)S(1)} %get-tuple-element.999), channel_id=1, source_target_pairs={{0,12},{2,14},{4,0},{6,2},{8,4},{10,6},{12,8},{14,10},{1,13},{3,15... | collective-permute-start | bytes 110600 | tf_op jit(solution)/shard_map/while/body/eval_jaxpr/ppermute | solution.py:29
  85.8 4.3 collective-permute-start.6
  95.9 17.4 %all-to-all-start = ((bf16[8,9,2048]{2,1,0:T(8,128)(2,1)}), bf16[8,9,2048]{2,1,0:T(8,128)(2,1)}, u32[]{:S(2)}, u32[]{:S(2)}) async-start(bf16[8,9,2048]{2,1,0:T(8,128)(2,1)} %reshape.247), calls=%async_computation | async-start | bytes 1048576 | tf_op jit(solution)/shard_map/while/body/eval_jaxpr/all_to_all | solution.py:111
  115.3 3.1 collective-permute-start.7
  122.9 7.1 %collective-permute-start = (bf16[1,1,9,2048]{3,2,0,1:T(8,128)(2,1)S(1)}, bf16[1,1,9,2048]{3,2,0,1:T(8,128)(2,1)}, u32[]{:S(2)}, u32[]{:S(2)}) collective-permute-start(bf16[1,1,9,2048]{3,2,0,1:T(8,128)(2,1)S(1)} %constant_dynamic-slice_fusion.26), channel_id=1, source_target_pairs={{0,2},{2,4},{4,6},{6,8},{8,10},{10,12},{12,14},{14,0},{1,3},{3,5},... | collective-permute-start | bytes 110600 | tf_op jit(solution)/shard_map/while/body/eval_jaxpr/ppermute | solution.py:29
  131.5 9.4 %collective-permute-start.1 = (bf16[1,1,9,2048]{3,2,0,1:T(8,128)(2,1)}, bf16[1,1,9,2048]{3,2,0,1:T(8,128)(2,1)S(1)}, u32[]{:S(2)}, u32[]{:S(2)}) collective-permute-start(bf16[1,1,9,2048]{3,2,0,1:T(8,128)(2,1)} %get-tuple-element.995), channel_id=1, source_target_pairs={{0,4},{2,6},{4,8},{6,10},{8,12},{10,14},{12,0},{14,2},{1,5},{3,7},... | collective-permute-start | bytes 110600 | tf_op jit(solution)/shard_map/while/body/eval_jaxpr/ppermute | solution.py:29
  133.3 8.2 %collective-permute-start.2 = (bf16[1,1,9,2048]{3,2,0,1:T(8,128)(2,1)S(1)}, bf16[1,1,9,2048]{3,2,0,1:T(8,128)(2,1)S(1)}, u32[]{:S(2)}, u32[]{:S(2)}) collective-permute-start(bf16[1,1,9,2048]{3,2,0,1:T(8,128)(2,1)S(1)} %get-tuple-element.996), channel_id=1, source_target_pairs={{0,6},{2,8},{4,10},{6,12},{8,14},{10,0},{12,2},{14,4},{1,7},{3,9},... | collective-permute-start | bytes 110600 | tf_op jit(solution)/shard_map/while/body/eval_jaxpr/ppermute | solution.py:29
  133.3 8.3 %collective-permute-start.3 = (bf16[1,1,9,2048]{3,2,0,1:T(8,128)(2,1)S(1)}, bf16[1,1,9,2048]{3,2,0,1:T(8,128)(2,1)S(1)}, u32[]{:S(2)}, u32[]{:S(2)}) collective-permute-start(bf16[1,1,9,2048]{3,2,0,1:T(8,128)(2,1)S(1)} %get-tuple-element.997), channel_id=1, source_target_pairs={{0,8},{2,10},{4,12},{6,14},{8,0},{10,2},{12,4},{14,6},{1,9},{3,11}... | collective-permute-start | bytes 110600 | tf_op jit(solution)/shard_map/while/body/eval_jaxpr/ppermute | solution.py:29
  135.8 5.9 collective-permute-start.4
  137.1 6.8 %collective-permute-start.5 = (bf16[1,1,9,2048]{3,2,0,1:T(8,128)(2,1)S(1)}, bf16[1,1,9,2048]{3,2,0,1:T(8,128)(2,1)S(1)}, u32[]{:S(2)}, u32[]{:S(2)}) collective-permute-start(bf16[1,1,9,2048]{3,2,0,1:T(8,128)(2,1)S(1)} %get-tuple-element.999), channel_id=1, source_target_pairs={{0,12},{2,14},{4,0},{6,2},{8,4},{10,6},{12,8},{14,10},{1,13},{3,15... | collective-permute-start | bytes 110600 | tf_op jit(solution)/shard_map/while/body/eval_jaxpr/ppermute | solution.py:29
  140.9 4.3 collective-permute-start.6
  151.0 17.4 %all-to-all-start = ((bf16[8,9,2048]{2,1,0:T(8,128)(2,1)}), bf16[8,9,2048]{2,1,0:T(8,128)(2,1)}, u32[]{:S(2)}, u32[]{:S(2)}) async-start(bf16[8,9,2048]{2,1,0:T(8,128)(2,1)} %reshape.247), calls=%async_computation | async-start | bytes 1048576 | tf_op jit(solution)/shard_map/while/body/eval_jaxpr/all_to_all | solution.py:111
  170.4 3.1 collective-permute-start.7
  178.0 7.1 %collective-permute-start = (bf16[1,1,9,2048]{3,2,0,1:T(8,128)(2,1)S(1)}, bf16[1,1,9,2048]{3,2,0,1:T(8,128)(2,1)}, u32[]{:S(2)}, u32[]{:S(2)}) collective-permute-start(bf16[1,1,9,2048]{3,2,0,1:T(8,128)(2,1)S(1)} %constant_dynamic-slice_fusion.26), channel_id=1, source_target_pairs={{0,2},{2,4},{4,6},{6,8},{8,10},{10,12},{12,14},{14,0},{1,3},{3,5},... | collective-permute-start | bytes 110600 | tf_op jit(solution)/shard_map/while/body/eval_jaxpr/ppermute | solution.py:29
  186.6 9.4 %collective-permute-start.1 = (bf16[1,1,9,2048]{3,2,0,1:T(8,128)(2,1)}, bf16[1,1,9,2048]{3,2,0,1:T(8,128)(2,1)S(1)}, u32[]{:S(2)}, u32[]{:S(2)}) collective-permute-start(bf16[1,1,9,2048]{3,2,0,1:T(8,128)(2,1)} %get-tuple-element.995), channel_id=1, source_target_pairs={{0,4},{2,6},{4,8},{6,10},{8,12},{10,14},{12,0},{14,2},{1,5},{3,7},... | collective-permute-start | bytes 110600 | tf_op jit(solution)/shard_map/while/body/eval_jaxpr/ppermute | solution.py:29
  188.3 8.2 %collective-permute-start.2 = (bf16[1,1,9,2048]{3,2,0,1:T(8,128)(2,1)S(1)}, bf16[1,1,9,2048]{3,2,0,1:T(8,128)(2,1)S(1)}, u32[]{:S(2)}, u32[]{:S(2)}) collective-permute-start(bf16[1,1,9,2048]{3,2,0,1:T(8,128)(2,1)S(1)} %get-tuple-element.996), channel_id=1, source_target_pairs={{0,6},{2,8},{4,10},{6,12},{8,14},{10,0},{12,2},{14,4},{1,7},{3,9},... | collective-permute-start | bytes 110600 | tf_op jit(solution)/shard_map/while/body/eval_jaxpr/ppermute | solution.py:29
  188.3 8.3 %collective-permute-start.3 = (bf16[1,1,9,2048]{3,2,0,1:T(8,128)(2,1)S(1)}, bf16[1,1,9,2048]{3,2,0,1:T(8,128)(2,1)S(1)}, u32[]{:S(2)}, u32[]{:S(2)}) collective-permute-start(bf16[1,1,9,2048]{3,2,0,1:T(8,128)(2,1)S(1)} %get-tuple-element.997), channel_id=1, source_target_pairs={{0,8},{2,10},{4,12},{6,14},{8,0},{10,2},{12,4},{14,6},{1,9},{3,11}... | collective-permute-start | bytes 110600 | tf_op jit(solution)/shard_map/while/body/eval_jaxpr/ppermute | solution.py:29
  190.9 5.9 collective-permute-start.4
  192.2 6.8 %collective-permute-start.5 = (bf16[1,1,9,2048]{3,2,0,1:T(8,128)(2,1)S(1)}, bf16[1,1,9,2048]{3,2,0,1:T(8,128)(2,1)S(1)}, u32[]{:S(2)}, u32[]{:S(2)}) collective-permute-start(bf16[1,1,9,2048]{3,2,0,1:T(8,128)(2,1)S(1)} %get-tuple-element.999), channel_id=1, source_target_pairs={{0,12},{2,14},{4,0},{6,2},{8,4},{10,6},{12,8},{14,10},{1,13},{3,15... | collective-permute-start | bytes 110600 | tf_op jit(solution)/shard_map/while/body/eval_jaxpr/ppermute | solution.py:29
  196.0 4.3 collective-permute-start.6
  206.1 17.3 %all-to-all-start = ((bf16[8,9,2048]{2,1,0:T(8,128)(2,1)}), bf16[8,9,2048]{2,1,0:T(8,128)(2,1)}, u32[]{:S(2)}, u32[]{:S(2)}) async-start(bf16[8,9,2048]{2,1,0:T(8,128)(2,1)} %reshape.247), calls=%async_computation | async-start | bytes 1048576 | tf_op jit(solution)/shard_map/while/body/eval_jaxpr/all_to_all | solution.py:111
  225.4 3.1 collective-permute-start.7
  233.0 7.1 %collective-permute-start = (bf16[1,1,9,2048]{3,2,0,1:T(8,128)(2,1)S(1)}, bf16[1,1,9,2048]{3,2,0,1:T(8,128)(2,1)}, u32[]{:S(2)}, u32[]{:S(2)}) collective-permute-start(bf16[1,1,9,2048]{3,2,0,1:T(8,128)(2,1)S(1)} %constant_dynamic-slice_fusion.26), channel_id=1, source_target_pairs={{0,2},{2,4},{4,6},{6,8},{8,10},{10,12},{12,14},{14,0},{1,3},{3,5},... | collective-permute-start | bytes 110600 | tf_op jit(solution)/shard_map/while/body/eval_jaxpr/ppermute | solution.py:29
  241.6 9.4 %collective-permute-start.1 = (bf16[1,1,9,2048]{3,2,0,1:T(8,128)(2,1)}, bf16[1,1,9,2048]{3,2,0,1:T(8,128)(2,1)S(1)}, u32[]{:S(2)}, u32[]{:S(2)}) collective-permute-start(bf16[1,1,9,2048]{3,2,0,1:T(8,128)(2,1)} %get-tuple-element.995), channel_id=1, source_target_pairs={{0,4},{2,6},{4,8},{6,10},{8,12},{10,14},{12,0},{14,2},{1,5},{3,7},... | collective-permute-start | bytes 110600 | tf_op jit(solution)/shard_map/while/body/eval_jaxpr/ppermute | solution.py:29
  243.4 8.2 %collective-permute-start.2 = (bf16[1,1,9,2048]{3,2,0,1:T(8,128)(2,1)S(1)}, bf16[1,1,9,2048]{3,2,0,1:T(8,128)(2,1)S(1)}, u32[]{:S(2)}, u32[]{:S(2)}) collective-permute-start(bf16[1,1,9,2048]{3,2,0,1:T(8,128)(2,1)S(1)} %get-tuple-element.996), channel_id=1, source_target_pairs={{0,6},{2,8},{4,10},{6,12},{8,14},{10,0},{12,2},{14,4},{1,7},{3,9},... | collective-permute-start | bytes 110600 | tf_op jit(solution)/shard_map/while/body/eval_jaxpr/ppermute | solution.py:29
  243.4 8.3 %collective-permute-start.3 = (bf16[1,1,9,2048]{3,2,0,1:T(8,128)(2,1)S(1)}, bf16[1,1,9,2048]{3,2,0,1:T(8,128)(2,1)S(1)}, u32[]{:S(2)}, u32[]{:S(2)}) collective-permute-start(bf16[1,1,9,2048]{3,2,0,1:T(8,128)(2,1)S(1)} %get-tuple-element.997), channel_id=1, source_target_pairs={{0,8},{2,10},{4,12},{6,14},{8,0},{10,2},{12,4},{14,6},{1,9},{3,11}... | collective-permute-start | bytes 110600 | tf_op jit(solution)/shard_map/while/body/eval_jaxpr/ppermute | solution.py:29
  245.9 5.9 collective-permute-start.4
  247.2 6.8 %collective-permute-start.5 = (bf16[1,1,9,2048]{3,2,0,1:T(8,128)(2,1)S(1)}, bf16[1,1,9,2048]{3,2,0,1:T(8,128)(2,1)S(1)}, u32[]{:S(2)}, u32[]{:S(2)}) collective-permute-start(bf16[1,1,9,2048]{3,2,0,1:T(8,128)(2,1)S(1)} %get-tuple-element.999), channel_id=1, source_target_pairs={{0,12},{2,14},{4,0},{6,2},{8,4},{10,6},{12,8},{14,10},{1,13},{3,15... | collective-permute-start | bytes 110600 | tf_op jit(solution)/shard_map/while/body/eval_jaxpr/ppermute | solution.py:29
  251.0 4.3 collective-permute-start.6
  261.1 17.4 %all-to-all-start = ((bf16[8,9,2048]{2,1,0:T(8,128)(2,1)}), bf16[8,9,2048]{2,1,0:T(8,128)(2,1)}, u32[]{:S(2)}, u32[]{:S(2)}) async-start(bf16[8,9,2048]{2,1,0:T(8,128)(2,1)} %reshape.247), calls=%async_computation | async-start | bytes 1048576 | tf_op jit(solution)/shard_map/while/body/eval_jaxpr/all_to_all | solution.py:111
  280.5 3.1 collective-permute-start.7
  297.3 17.9 %all-to-all-start.1 = ((bf16[8,9,2048]{2,1,0:T(8,128)(2,1)}), bf16[8,9,2048]{2,1,0:T(8,128)(2,1)S(1)}, u32[]{:S(2)}, u32[]{:S(2)}) async-start(bf16[8,9,2048]{2,1,0:T(8,128)(2,1)} %reshape.250), calls=%async_computation.1 | async-start | bytes 1048576 | tf_op jit(solution)/shard_map/while/body/eval_jaxpr/all_to_all | solution.py:175
  325.1 18.3 %all-to-all-start.2 = ((bf16[8,9,2048]{2,1,0:T(8,128)(2,1)}), bf16[8,9,2048]{2,1,0:T(8,128)(2,1)}, u32[]{:S(2)}, u32[]{:S(2)}) async-start(bf16[8,9,2048]{2,1,0:T(8,128)(2,1)} %reshape.252), calls=%async_computation.2 | async-start | bytes 1048576 | tf_op jit(solution)/shard_map/while/body/eval_jaxpr/all_to_all | solution.py:186
  346.8 3.2 collective-permute-start.8
  353.7 19.4 %all-to-all-start.1 = ((bf16[8,9,2048]{2,1,0:T(8,128)(2,1)}), bf16[8,9,2048]{2,1,0:T(8,128)(2,1)S(1)}, u32[]{:S(2)}, u32[]{:S(2)}) async-start(bf16[8,9,2048]{2,1,0:T(8,128)(2,1)} %reshape.250), calls=%async_computation.1 | async-start | bytes 1048576 | tf_op jit(solution)/shard_map/while/body/eval_jaxpr/all_to_all | solution.py:175
  383.0 19.0 %all-to-all-start.2 = ((bf16[8,9,2048]{2,1,0:T(8,128)(2,1)}), bf16[8,9,2048]{2,1,0:T(8,128)(2,1)}, u32[]{:S(2)}, u32[]{:S(2)}) async-start(bf16[8,9,2048]{2,1,0:T(8,128)(2,1)} %reshape.252), calls=%async_computation.2 | async-start | bytes 1048576 | tf_op jit(solution)/shard_map/while/body/eval_jaxpr/all_to_all | solution.py:186
  405.4 3.2 collective-permute-start.8
  412.3 19.4 %all-to-all-start.1 = ((bf16[8,9,2048]{2,1,0:T(8,128)(2,1)}), bf16[8,9,2048]{2,1,0:T(8,128)(2,1)S(1)}, u32[]{:S(2)}, u32[]{:S(2)}) async-start(bf16[8,9,2048]{2,1,0:T(8,128)(2,1)} %reshape.250), calls=%async_computation.1 | async-start | bytes 1048576 | tf_op jit(solution)/shard_map/while/body/eval_jaxpr/all_to_all | solution.py:175
  441.6 19.0 %all-to-all-start.2 = ((bf16[8,9,2048]{2,1,0:T(8,128)(2,1)}), bf16[8,9,2048]{2,1,0:T(8,128)(2,1)}, u32[]{:S(2)}, u32[]{:S(2)}) async-start(bf16[8,9,2048]{2,1,0:T(8,128)(2,1)} %reshape.252), calls=%async_computation.2 | async-start | bytes 1048576 | tf_op jit(solution)/shard_map/while/body/eval_jaxpr/all_to_all | solution.py:186
  446.7 18.7 %copy-start.6 = (bf16[1,72,2048]{2,1,0:T(8,128)(2,1)S(1)}, bf16[1,72,2048]{2,1,0:T(8,128)(2,1)}, u32[]{:S(2)}) copy-start(bf16[1,72,2048]{2,1,0:T(8,128)(2,1)} %reshape.254) | copy-start | bytes 884740 | tf_op jit(solution)/shard_map/while
  464.0 3.2 collective-permute-start.8
  471.0 19.4 %all-to-all-start.1 = ((bf16[8,9,2048]{2,1,0:T(8,128)(2,1)}), bf16[8,9,2048]{2,1,0:T(8,128)(2,1)S(1)}, u32[]{:S(2)}, u32[]{:S(2)}) async-start(bf16[8,9,2048]{2,1,0:T(8,128)(2,1)} %reshape.250), calls=%async_computation.1 | async-start | bytes 1048576 | tf_op jit(solution)/shard_map/while/body/eval_jaxpr/all_to_all | solution.py:175
  500.3 19.0 %all-to-all-start.2 = ((bf16[8,9,2048]{2,1,0:T(8,128)(2,1)}), bf16[8,9,2048]{2,1,0:T(8,128)(2,1)}, u32[]{:S(2)}, u32[]{:S(2)}) async-start(bf16[8,9,2048]{2,1,0:T(8,128)(2,1)} %reshape.252), calls=%async_computation.2 | async-start | bytes 1048576 | tf_op jit(solution)/shard_map/while/body/eval_jaxpr/all_to_all | solution.py:186
  522.7 3.2 collective-permute-start.8
  529.6 19.4 %all-to-all-start.1 = ((bf16[8,9,2048]{2,1,0:T(8,128)(2,1)}), bf16[8,9,2048]{2,1,0:T(8,128)(2,1)S(1)}, u32[]{:S(2)}, u32[]{:S(2)}) async-start(bf16[8,9,2048]{2,1,0:T(8,128)(2,1)} %reshape.250), calls=%async_computation.1 | async-start | bytes 1048576 | tf_op jit(solution)/shard_map/while/body/eval_jaxpr/all_to_all | solution.py:175
  558.9 19.0 %all-to-all-start.2 = ((bf16[8,9,2048]{2,1,0:T(8,128)(2,1)}), bf16[8,9,2048]{2,1,0:T(8,128)(2,1)}, u32[]{:S(2)}, u32[]{:S(2)}) async-start(bf16[8,9,2048]{2,1,0:T(8,128)(2,1)} %reshape.252), calls=%async_computation.2 | async-start | bytes 1048576 | tf_op jit(solution)/shard_map/while/body/eval_jaxpr/all_to_all | solution.py:186
  581.3 3.2 collective-permute-start.8
  584.5 40.1 %all-to-all-start.3 = ((bf16[288,2,1024]{2,0,1:T(8,128)(2,1)}), bf16[288,2,1024]{2,0,1:T(8,128)(2,1)}, u32[]{:S(2)}, u32[]{:S(2)}) async-start(bf16[288,2,1024]{2,0,1:T(8,128)(2,1)} %copy.40), calls=%async_computation.3 | async-start | bytes 2359296 | tf_op jit(solution)/shard_map/all_to_all | solution.py:226
  590.1 23.4 %copy-start.9 = (bf16[4,72,640]{2,1,0:T(8,128)(2,1)S(1)}, bf16[4,72,640]{2,1,0:T(8,128)(2,1)}, u32[]{:S(2)}) copy-start(bf16[4,72,640]{2,1,0:T(8,128)(2,1)} %get-tuple-element.700) | copy-start | bytes 1105924
  624.7 34.6 %all-to-all-start.4 = ((bf16[288,2,1024]{2,0,1:T(8,128)(2,1)}), bf16[288,2,1024]{2,0,1:T(8,128)(2,1)S(1)}, u32[]{:S(2)}, u32[]{:S(2)}) async-start(bf16[288,2,1024]{2,0,1:T(8,128)(2,1)} %copy.41), calls=%async_computation.4 | async-start | bytes 2359296 | tf_op jit(solution)/shard_map/all_to_all | solution.py:227
  (39 other events, 206.6 us)
